TPU v7x, 32 devices: a whole 2x2x4 slice. The times are simulated.
32 devices in a mesh: groups: 2 (over y), ctx: 8 (over z, x), head: 2 (over core).
Axes of the slice: x: 2, y: 2, z: 4, core: 2. Of those that a mesh axis runs over, the one named last changes fastest.
Arguments:
- query_tensor: bfloat16 [2048, 4096], P(('groups', 'ctx'), 'head'), parts along dimension 0, may hold values from -110 to 110
- key_tensor: bfloat16 [2048, 1024], P(('groups', 'ctx'), 'head'), parts along dimension 0, may hold values from -6 to 6
- value_tensor: bfloat16 [2048, 1024], P(('groups', 'ctx'), 'head'), parts along dimension 0, may hold values from -6 to 6
- slash_offsets: int32 [16, 2], P(('groups', 'head')), parts along dimension 0, may hold values from 256 to 1023
- vertical_tiles: int32 [16, 2], P(('groups', 'head')), parts along dimension 0, may hold values from 0 to 7, as said below
- kept_rows: int32 [16, 32], P(('groups', 'ctx')), parts along dimension 0, may hold values from 0 to 127, as said below
- kept_count: int32 [16], P('groups'), parts along dimension 0, may hold values from 4 to 32, as said below
- out_weight: bfloat16 [2048, 4096], P('ctx', 'head'), may hold values from -0.09375 to 0.09375
Outputs:
- attended: bfloat16 [2048, 4096], P(('groups', 'ctx'), 'head'), parts along dimension 0
- projected: bfloat16 [256, 2048], P(('groups', 'ctx'), 'head'), parts along dimension 0
There are 2 independent parts, one for each index of `groups`. A program takes and returns all parts, laid end to end along the dimension named above; an argument that names none is the same for every part. Nothing has to cross between parts.
Inputs may be any that keep to these rules, and one draw needn't show every extreme that they name: `vertical_tiles`: the tiles of one KV head differ. `kept_rows`: row c holds distinct local row indices of shard c; its first kept_count[c] entries are the kept rows in increasing order, the other entries are not kept. `kept_count`: each aligned block of 4 consecutive shards keeps exactly 64 rows in all.
All inputs are finite; a program needn't handle non-finite values.
Results may differ from a plain program's by a relative error of at most 0.0056.
Values may be sent and summed in bfloat16 or wider, within the bound.
No kernel may reach another device: no remote copies, remote signals or barrier semaphores. Data moves between devices by JAX's collectives and lax.ppermute only.
A program may use at most 64 MiB of HBM per device.

v0:
```python
import jax
import jax.numpy as jnp
from jax import lax
from jax.sharding import PartitionSpec as P

HEAD_SIZE = 128
SLASH_SPAN = 8
VTILES = 2
LOCAL_BAND_KEYS = 256
SLASH_W = 128
VTILE = 128


def shifted_2(x, axis, by):
    size = lax.axis_size(axis)
    pairs = [(i, i + by) for i in range(size) if 0 <= i + by < size]
    return lax.ppermute(x, axis, pairs)


def broadcast(x, axis, root):
    mine = lax.axis_index(axis) == root
    return lax.psum(jnp.where(mine, x, jnp.zeros_like(x)), axis)


def attend(
    query_rows,
    key_slab,
    value_slab,
    key_pos,
    query_pos,
    slash_shift_list,
    tile_list,
    column_kind,
    group_width,
):
    scores = jnp.dot(query_rows, key_slab.T, preferred_element_type=jnp.float32) * key_slab.shape[
        -1
    ] ** (-0.5)
    distance = query_pos[:, None] - key_pos[None, :]
    key_tile = jnp.where(key_pos >= 0, key_pos // VTILE, -1)
    vertical = jnp.any(key_tile[:, None] == tile_list[None, :], axis=1)[None, :]
    in_band = (distance >= 0) & (distance < LOCAL_BAND_KEYS) & ~vertical
    first_slash = (
        (distance >= slash_shift_list[0]) & (distance < slash_shift_list[0] + SLASH_W) & ~vertical
    )
    second_slash = (
        (distance >= slash_shift_list[1]) & (distance < slash_shift_list[1] + SLASH_W) & ~vertical
    )
    earlier = in_band | first_slash
    kinds = column_kind[None, :]
    allowed = jnp.where(
        kinds == 0,
        in_band,
        jnp.where(
            kinds == 1,
            first_slash & ~in_band,
            jnp.where(kinds == 2, second_slash & ~earlier, distance >= 0),
        ),
    )
    allowed = jnp.tile(allowed & (key_pos >= 0)[None, :], (group_width, 1))
    masked = jnp.where(allowed, scores, -jnp.inf)
    row_max = jnp.max(masked, axis=1, keepdims=True)
    weights = jnp.where(allowed, jnp.exp(masked - row_max), 0.0)
    row_sum = jnp.sum(weights, axis=1, keepdims=True)
    blended = jnp.dot(weights.astype(jnp.bfloat16), value_slab, preferred_element_type=jnp.float32)
    return (blended / row_sum).astype(jnp.bfloat16)


def heads_first(stacked, local_heads, head_dim):
    reordered = jnp.moveaxis(stacked, -2, 0)
    return reordered.reshape(local_heads, -1, head_dim)


def move_near(row_block, is_live, offset, target_slot, keep_rows, sender):
    slot_grid = jnp.arange(keep_rows, dtype=jnp.int32)[:, None]
    gathered = jnp.zeros((keep_rows, row_block.shape[1]), jnp.float32)
    for travel in range(-3, 4):
        chooser = (
            (slot_grid == target_slot[None, :]) & (offset[None, :] == travel) & is_live[None, :]
        ).astype(jnp.bfloat16)
        parcel = jnp.dot(chooser, row_block, preferred_element_type=jnp.float32).astype(
            jnp.bfloat16
        )
        if travel != 0:
            parcel = sender(parcel, travel)
        gathered = gathered + parcel.astype(jnp.float32)
    return gathered.astype(jnp.bfloat16)


def local(
    query_tensor,
    key_tensor,
    value_tensor,
    slash_offsets,
    vertical_tiles,
    kept_rows,
    kept_count,
    out_weight,
):
    shard_length = query_tensor.shape[0]
    head_dim = HEAD_SIZE
    local_heads = key_tensor.shape[1] // head_dim
    group_width = query_tensor.shape[1] // key_tensor.shape[1]
    shard_index = lax.axis_index("ctx")
    first_pos = shard_index * shard_length
    key_heads = key_tensor.reshape(shard_length, local_heads, head_dim)
    value_heads = value_tensor.reshape(shard_length, local_heads, head_dim)
    slash_spans = slash_offsets // shard_length
    own_pair = jnp.stack([key_heads, value_heads])
    moving = jnp.concatenate([own_pair, own_pair], 0)
    member_spans = jnp.stack(
        [slash_spans[:, 0], slash_spans[:, 0], slash_spans[:, 1], slash_spans[:, 1]]
    )
    for bit_number in range((SLASH_SPAN - 1).bit_length()):
        shifted = shifted_2(moving, "ctx", 1 << bit_number)
        head_flags = (member_spans >> bit_number & 1 == 1)[:, None, :, None]
        moving = jnp.where(head_flags, shifted, moving)
    nearby = jnp.concatenate([moving, own_pair], 0)
    distances = [nearby]
    for repeat_factor in range(2):
        nearby = shifted_2(nearby, "ctx", 1)
        distances.append(nearby)
    ordered = jnp.stack([distances[2], distances[1], distances[0]])
    band_pieces = ordered[:, 4:6]
    slash_pieces = jnp.stack([ordered[:, 0:2], ordered[:, 2:4]])
    tile_keys = []
    tile_values = []
    for head_number in range(local_heads):
        for tile_index in range(VTILES):
            fetched = broadcast(
                jnp.stack([key_heads[:, head_number], value_heads[:, head_number]]),
                "ctx",
                vertical_tiles[head_number, tile_index],
            )
            tile_keys.append(fetched[0])
            tile_values.append(fetched[1])
    all_keys = jnp.concatenate(
        [
            heads_first(band_pieces[:, 0], local_heads, head_dim),
            heads_first(slash_pieces[:, :, 0], local_heads, head_dim),
            jnp.stack(tile_keys).reshape(local_heads, VTILES * shard_length, head_dim),
        ],
        1,
    )
    all_values = jnp.concatenate(
        [
            heads_first(band_pieces[:, 1], local_heads, head_dim),
            heads_first(slash_pieces[:, :, 1], local_heads, head_dim),
            jnp.stack(tile_values).reshape(local_heads, VTILES * shard_length, head_dim),
        ],
        1,
    )
    window = jnp.arange(3 * shard_length, dtype=jnp.int32)
    band_pos = jnp.broadcast_to(
        first_pos - 2 * shard_length + window, (local_heads, 3 * shard_length)
    )
    slash_pos = first_pos - (slash_spans[:, :, None] + 2) * shard_length + window[None, None, :]
    tile_pos = (
        vertical_tiles[:, :, None] * shard_length
        + jnp.arange(shard_length, dtype=jnp.int32)[None, None, :]
    )
    key_pos = jnp.concatenate(
        [band_pos, slash_pos.reshape(local_heads, -1), tile_pos.reshape(local_heads, -1)], 1
    )
    column_kind = jnp.concatenate(
        [
            jnp.full((3 * shard_length,), 0, jnp.int32),
            jnp.full((3 * shard_length,), 1, jnp.int32),
            jnp.full((3 * shard_length,), 2, jnp.int32),
            jnp.full((VTILES * shard_length,), 3, jnp.int32),
        ]
    )
    query_pos = first_pos + jnp.arange(shard_length, dtype=jnp.int32)
    query_heads = (
        query_tensor.reshape(shard_length, local_heads, group_width, head_dim)
        .transpose(1, 2, 0, 3)
        .reshape(local_heads, group_width * shard_length, head_dim)
    )

    def attend_head(packed):
        return attend(
            packed[0],
            packed[1],
            packed[2],
            packed[3],
            query_pos,
            packed[4],
            packed[5],
            column_kind,
            group_width,
        )

    mixed_heads = lax.map(
        attend_head, (query_heads, all_keys, all_values, key_pos, slash_offsets, vertical_tiles)
    )
    attended = (
        mixed_heads.reshape(local_heads, group_width, shard_length, head_dim)
        .transpose(2, 0, 1, 3)
        .reshape(shard_length, -1)
    )
    keep_rows = shard_length // 8
    capacity = kept_rows.shape[1]
    starts = jnp.cumsum(kept_count) - kept_count
    slot_ids = jnp.arange(capacity, dtype=jnp.int32)
    is_live = slot_ids < kept_count[shard_index]
    placed_at = starts[shard_index] + slot_ids
    target_shard = placed_at // keep_rows
    target_slot = placed_at % keep_rows
    offset = target_shard - shard_index
    selected = jnp.take(attended, kept_rows[0], axis=0)
    rounded = lax.psum_scatter(
        lax.dot_general(
            selected,
            lax.all_gather(out_weight, "ctx", axis=0, tiled=True),
            (((1,), (1,)), ((), ())),
            preferred_element_type=jnp.float32,
        ),
        "head",
        scatter_dimension=1,
        tiled=True,
    ).astype(jnp.bfloat16)

    def send_output(parcel, travel):
        return shifted_2(parcel, "ctx", travel)

    projected = move_near(rounded, is_live, offset, target_slot, keep_rows, send_output)
    return (attended, projected)


def solution(mesh):
    placed = (
        P(("groups", "ctx"), "head"),
        P(("groups", "ctx"), "head"),
        P(("groups", "ctx"), "head"),
        P(("groups", "head"), None),
        P(("groups", "head"), None),
        P(("groups", "ctx"), None),
        P("groups"),
        P("ctx", "head"),
    )
    return jax.shard_map(
        local,
        mesh=mesh,
        in_specs=placed,
        out_specs=(P(("groups", "ctx"), "head"), P(("groups", "ctx"), "head")),
        check_vma=False,
    )
```

profile of v0, /device:TPU:16, one launch (start us, length us, event | category | flops | bytes accessed | tf_op | source)
XLA Modules:
  0.0 286.8 jit_solution(2545705615501974319)
XLA Ops:
  7.2 1.6 fusion.89
  20.1 3.4 %collective-permute-start = (bf16[4,128,4,128]{3,1,2,0:T(8,128)(2,1)S(1)}, bf16[4,128,4,128]{3,1,2,0:T(8,128)(2,1)S(1)}, u32[]{:S(2)}, u32[]{:S(2)}) collective-permute-start(bf16[4,128,4,128]{3,1,2,0:T(8,128)(2,1)S(1)} %get-tuple-element.200), channel_id=1, source_target_pairs={{0,2},{2,4},{4,6},{6,8},{8,10},{10,12},{12,14},{1,3},{3,5},{5,7},{... | collective-permute-start | bytes 1572872 | tf_op jit(solution)/shard_map/ppermute | solution.py:17
  26.1 16.1 %collective-permute-done = bf16[4,128,4,128]{3,1,2,0:T(8,128)(2,1)S(1)} collective-permute-done((bf16[4,128,4,128]{3,1,2,0:T(8,128)(2,1)S(1)}, bf16[4,128,4,128]{3,1,2,0:T(8,128)(2,1)S(1)}, u32[]{:S(2)}, u32[]{:S(2)}) %collective-permute-start) | collective-permute-done | bytes 524320 | tf_op jit(solution)/shard_map/ppermute | solution.py:17
  42.3 3.6 %collective-permute-start.1 = (bf16[4,128,4,128]{3,1,2,0:T(8,128)(2,1)S(1)}, bf16[4,128,4,128]{3,1,2,0:T(8,128)(2,1)S(1)}, u32[]{:S(2)}, u32[]{:S(2)}) collective-permute-start(bf16[4,128,4,128]{3,1,2,0:T(8,128)(2,1)S(1)} %broadcast_select_fusion), channel_id=1, source_target_pairs={{0,4},{2,6},{4,8},{6,10},{8,12},{10,14},{1,5},{3,7},{5,9},{7,11},{... | collective-permute-start | bytes 1572872 | tf_op jit(solution)/shard_map/ppermute | solution.py:17
  46.0 12.5 %collective-permute-done.1 = bf16[4,128,4,128]{3,1,2,0:T(8,128)(2,1)S(1)} collective-permute-done((bf16[4,128,4,128]{3,1,2,0:T(8,128)(2,1)S(1)}, bf16[4,128,4,128]{3,1,2,0:T(8,128)(2,1)S(1)}, u32[]{:S(2)}, u32[]{:S(2)}) %collective-permute-start.1) | collective-permute-done | bytes 524320 | tf_op jit(solution)/shard_map/ppermute | solution.py:17
  58.7 1.3 collective-permute-start.2
  60.6 14.7 %collective-permute-done.2 = bf16[4,128,4,128]{3,1,2,0:T(8,128)(2,1)S(1)} collective-permute-done((bf16[4,128,4,128]{3,1,2,0:T(8,128)(2,1)S(1)}, bf16[4,128,4,128]{3,1,2,0:T(8,128)(2,1)S(1)}, u32[]{:S(2)}, u32[]{:S(2)}) %collective-permute-start.2) | collective-permute-done | bytes 524320 | tf_op jit(solution)/shard_map/ppermute | solution.py:17
  75.6 1.9 collective-permute-start.3
  77.5 21.4 %all-reduce.3.cloned.1.call-done = (bf16[2,128,128]{2,1,0:T(8,128)(2,1)}, bf16[2,128,128]{2,1,0:T(8,128)(2,1)}, bf16[2,128,128]{2,1,0:T(8,128)(2,1)}, bf16[2,128...) async-done(((bf16[2,128,128]{2,1,0:T(8,128)(2,1)}, ...) | async-done | bytes 524304 | tf_op jit(solution)/shard_map/psum | solution.py:22
  102.1 6.4 %collective-permute-done.3 = bf16[6,128,4,128]{3,1,2,0:T(8,128)(2,1)S(1)} collective-permute-done((bf16[6,128,4,128]{3,1,2,0:T(8,128)(2,1)S(1)}, bf16[6,128,4,128]{3,1,2,0:T(8,128)(2,1)S(1)}, u32[]{:S(2)}, u32[]{:S(2)}) %collective-permute-start.3) | collective-permute-done | bytes 786464 | tf_op jit(solution)/shard_map/ppermute | solution.py:17
  108.5 5.1 %collective-permute-start.4 = (bf16[6,128,4,128]{3,1,2,0:T(8,128)(2,1)S(1)}, bf16[6,128,4,128]{3,1,2,0:T(8,128)(2,1)S(1)}, u32[]{:S(2)}, u32[]{:S(2)}) collective-permute-start(bf16[6,128,4,128]{3,1,2,0:T(8,128)(2,1)S(1)} %collective-permute-done.3), channel_id=1, source_target_pairs={{0,2},{2,4},{4,6},{6,8},{8,10},{10,12},{12,14},{1,3},{3,5},{5,7},{... | collective-permute-start | bytes 2359304 | tf_op jit(solution)/shard_map/ppermute | solution.py:17
  116.7 46.3 %collective-permute-done.4 = bf16[6,128,4,128]{3,1,2,0:T(8,128)(2,1)S(1)} collective-permute-done((bf16[6,128,4,128]{3,1,2,0:T(8,128)(2,1)S(1)}, bf16[6,128,4,128]{3,1,2,0:T(8,128)(2,1)S(1)}, u32[]{:S(2)}, u32[]{:S(2)}) %collective-permute-start.4) | collective-permute-done | bytes 786464 | tf_op jit(solution)/shard_map/ppermute | solution.py:17
  164.4 27.8 %while.13 = (s32[]{:T(128)}, bf16[4,512,128]{2,1,0:T(8,128)(2,1)}, s32[4,1408]{1,0:T(4,128)S(1)}, s32[4,2]{1,0:T(4,128)S(1)}, s32[4,2]{0,1:T(2,128)S(1)}, /*inde...) while((s32[]{:T(128)}, bf16[4,512,128]{2,1,0:T(8,128)(2,1)}, ...), condition=%wide.region_12.13_spmd.clone, body=%wide.region_8.12_spmd.clone.sunk | while | flops 378271104 | bytes 10238073 | solution.py:193
  166.5 2.0 fusion.113
  170.1 1.2 fusion.116
  173.4 2.0 fusion.113
  177.1 1.2 fusion.116
  180.4 2.0 fusion.113
  184.0 1.2 fusion.116
  187.3 2.0 fusion.113
  191.0 1.2 fusion.116
  192.2 1.4 copy.80
  194.7 46.6 %all-gather.2.cloned.1.call-done = bf16[2048,2048]{1,0:T(8,128)(2,1)} async-done(((bf16[256,2048]{1,0:T(8,128)(2,1)}), bf16[2048,2048]{1,0:T(8,128)(2,1)}) %all-gather.2.cloned.1.call-update) | async-done | bytes 8388624 | tf_op jit(solution)/shard_map/all_gather | solution.py:214
  241.3 6.7 %fusion.32 = f32[32,2048]{1,0:T(8,128)} fusion(bf16[2048,2048]{1,0:T(8,128)(2,1)} %all-gather.2.cloned.1.call-done, bf16[32,2048]{1,0:T(8,128)(2,1)S(1)} %gather_fusion, pred[32]{0:T(512)(128)(4,1)S(1)} %compare_and_fusion), kind=kOutput, calls=%fused_computation.75 | convolution fusion | flops 268500992 | bytes 8781856 | tf_op jit(solution)/shard_map/dot_general | solution.py:212
  250.0 5.2 %reduce-scatter.2.cloned.1.call-done = f32[32,1024]{1,0:T(8,128)} async-done(((f32[32,2048]{1,0:T(8,128)}), f32[32,1024]{1,0:T(8,128)}) %reduce-scatter.2.cloned.1.call-update) | async-done | bytes 131088 | tf_op jit(solution)/shard_map/reduce_scatter | solution.py:211
  256.2 3.3 %collective-permute-start.5 = (bf16[16,1024]{1,0:T(8,128)(2,1)S(1)}, bf16[16,1024]{1,0:T(8,128)(2,1)S(1)}, u32[]{:S(2)}, u32[]{:S(2)}) collective-permute-start(bf16[16,1024]{1,0:T(8,128)(2,1)S(1)} %convolution_convert_fusion.6), channel_id=1, source_target_pairs={{6,0},{8,2},{10,4},{12,6},{14,8},{7,1},{9,3},{11,5},{13,7},{15,9},... | collective-permute-start | bytes 98312 | tf_op jit(solution)/shard_map/ppermute | solution.py:17
  259.7 1.9 collective-permute-start.6
  261.8 2.2 collective-permute-start.7
  264.1 3.6 %collective-permute-start.8 = (bf16[16,1024]{1,0:T(8,128)(2,1)S(1)}, bf16[16,1024]{1,0:T(8,128)(2,1)S(1)}, u32[]{:S(2)}, u32[]{:S(2)}) collective-permute-start(bf16[16,1024]{1,0:T(8,128)(2,1)S(1)} %convolution_convert_fusion.2), channel_id=1, source_target_pairs={{0,2},{2,4},{4,6},{6,8},{8,10},{10,12},{12,14},{1,3},{3,5},{5,7},{... | collective-permute-start | bytes 98312 | tf_op jit(solution)/shard_map/ppermute | solution.py:17
  267.9 3.9 %collective-permute-start.9 = (bf16[16,1024]{1,0:T(8,128)(2,1)S(1)}, bf16[16,1024]{1,0:T(8,128)(2,1)S(1)}, u32[]{:S(2)}, u32[]{:S(2)}) collective-permute-start(bf16[16,1024]{1,0:T(8,128)(2,1)S(1)} %convolution_convert_fusion.1), channel_id=1, source_target_pairs={{0,4},{2,6},{4,8},{6,10},{8,12},{10,14},{1,5},{3,7},{5,9},{7,11},{... | collective-permute-start | bytes 98312 | tf_op jit(solution)/shard_map/ppermute | solution.py:17
  271.9 1.9 collective-permute-start.10
  273.9 5.6 %collective-permute-done.10 = bf16[16,1024]{1,0:T(8,128)(2,1)S(1)} collective-permute-done((bf16[16,1024]{1,0:T(8,128)(2,1)S(1)}, bf16[16,1024]{1,0:T(8,128)(2,1)S(1)}, u32[]{:S(2)}, u32[]{:S(2)}) %collective-permute-start.10) | collective-permute-done | bytes 32800 | tf_op jit(solution)/shard_map/ppermute | solution.py:17
  (157 shorter events, 32.7 us)
Async XLA Ops:
  7.2 91.8 %all-reduce.3.cloned.1.call-start = ((), (), s32[]{:S(2)}) async-start(), calls=%async_computation.3 | async-start | bytes 1048576 | tf_op jit(solution)/shard_map/psum | solution.py:22
  10.2 9.6 %copy-start.2 = (bf16[128,512]{1,0:T(8,128)(2,1)S(1)}, bf16[128,512]{1,0:T(8,128)(2,1)}, u32[]{:S(2)}) copy-start(bf16[128,512]{1,0:T(8,128)(2,1)} %param.11) | copy-start | bytes 393220
  11.1 8.7 %copy-start.3 = (bf16[128,512]{1,0:T(8,128)(2,1)S(1)}, bf16[128,512]{1,0:T(8,128)(2,1)}, u32[]{:S(2)}) copy-start(bf16[128,512]{1,0:T(8,128)(2,1)} %param.12) | copy-start | bytes 393220
  16.2 7.3 %copy-start.8 = (s32[4,2]{0,1:T(2,128)S(1)}, s32[4,2]{0,1:T(2,128)}, u32[]{:S(2)}) copy-start(s32[4,2]{0,1:T(2,128)} %param.14) | copy-start | bytes 100
  16.2 7.4 %copy-start.9 = (s32[4,2]{0,1:T(2,128)S(1)}, s32[4,2]{0,1:T(2,128)}, u32[]{:S(2)}) copy-start(s32[4,2]{0,1:T(2,128)} %param.13) | copy-start | bytes 100
  16.2 7.7 %copy-start.1 = (bf16[128,2048]{1,0:T(8,128)(2,1)S(1)}, bf16[128,2048]{1,0:T(8,128)(2,1)}, u32[]{:S(2)}) copy-start(bf16[128,2048]{1,0:T(8,128)(2,1)} %param.10) | copy-start | bytes 1572868
  19.0 5.5 %copy-start.10 = (s32[8]{0:T(128)S(1)}, s32[8]{0:T(128)}, u32[]{:S(2)}) copy-start(s32[8]{0:T(128)} %param.16) | copy-start | bytes 100
  19.0 7.0 %copy-start.11 = (s32[1,32]{1,0:T(1,128)S(1)}, s32[1,32]{1,0:T(1,128)}, u32[]{:S(2)}) copy-start(s32[1,32]{1,0:T(1,128)} %param.15) | copy-start | bytes 388
  19.0 222.3 %all-gather.2.cloned.1.call-start = ((), (), s32[]{:S(2)}) async-start(), calls=%async_computation.1 | async-start | bytes 9437184 | tf_op jit(solution)/shard_map/all_gather | solution.py:214
  19.7 235.5 %reduce-scatter.2.cloned.1.call-start = ((), (), s32[]{:S(2)}) async-start(), calls=%async_computation.2 | async-start | bytes 393216 | tf_op jit(solution)/shard_map/reduce_scatter | solution.py:211
  20.1 22.1 %collective-permute-start = (bf16[4,128,4,128]{3,1,2,0:T(8,128)(2,1)S(1)}, bf16[4,128,4,128]{3,1,2,0:T(8,128)(2,1)S(1)}, u32[]{:S(2)}, u32[]{:S(2)}) collective-permute-start(bf16[4,128,4,128]{3,1,2,0:T(8,128)(2,1)S(1)} %get-tuple-element.200), channel_id=1, source_target_pairs={{0,2},{2,4},{4,6},{6,8},{8,10},{10,12},{12,14},{1,3},{3,5},{5,7},{... | collective-permute-start | bytes 1572872 | tf_op jit(solution)/shard_map/ppermute | solution.py:17
  42.3 16.2 %collective-permute-start.1 = (bf16[4,128,4,128]{3,1,2,0:T(8,128)(2,1)S(1)}, bf16[4,128,4,128]{3,1,2,0:T(8,128)(2,1)S(1)}, u32[]{:S(2)}, u32[]{:S(2)}) collective-permute-start(bf16[4,128,4,128]{3,1,2,0:T(8,128)(2,1)S(1)} %broadcast_select_fusion), channel_id=1, source_target_pairs={{0,4},{2,6},{4,8},{6,10},{8,12},{10,14},{1,5},{3,7},{5,9},{7,11},{... | collective-permute-start | bytes 1572872 | tf_op jit(solution)/shard_map/ppermute | solution.py:17
  58.7 16.7 %collective-permute-start.2 = (bf16[4,128,4,128]{3,1,2,0:T(8,128)(2,1)S(1)}, bf16[4,128,4,128]{3,1,2,0:T(8,128)(2,1)S(1)}, u32[]{:S(2)}, u32[]{:S(2)}) collective-permute-start(bf16[4,128,4,128]{3,1,2,0:T(8,128)(2,1)S(1)} %broadcast_select_fusion.1), channel_id=1, source_target_pairs={{0,8},{2,10},{4,12},{6,14},{1,9},{3,11},{5,13},{7,15},{16,24},{18,... | collective-permute-start | bytes 1572872 | tf_op jit(solution)/shard_map/ppermute | solution.py:17
  75.6 32.9 %collective-permute-start.3 = (bf16[6,128,4,128]{3,1,2,0:T(8,128)(2,1)S(1)}, bf16[6,128,4,128]{3,1,2,0:T(8,128)(2,1)S(1)}, u32[]{:S(2)}, u32[]{:S(2)}) collective-permute-start(bf16[6,128,4,128]{3,1,2,0:T(8,128)(2,1)S(1)} %get-tuple-element.198), channel_id=1, source_target_pairs={{0,2},{2,4},{4,6},{6,8},{8,10},{10,12},{12,14},{1,3},{3,5},{5,7},{... | collective-permute-start | bytes 2359304 | tf_op jit(solution)/shard_map/ppermute | solution.py:17
  108.5 54.5 %collective-permute-start.4 = (bf16[6,128,4,128]{3,1,2,0:T(8,128)(2,1)S(1)}, bf16[6,128,4,128]{3,1,2,0:T(8,128)(2,1)S(1)}, u32[]{:S(2)}, u32[]{:S(2)}) collective-permute-start(bf16[6,128,4,128]{3,1,2,0:T(8,128)(2,1)S(1)} %collective-permute-done.3), channel_id=1, source_target_pairs={{0,2},{2,4},{4,6},{6,8},{8,10},{10,12},{12,14},{1,3},{3,5},{5,7},{... | collective-permute-start | bytes 2359304 | tf_op jit(solution)/shard_map/ppermute | solution.py:17
  163.6 0.7 copy-start.4
  163.6 0.7 copy-start.5
  163.6 0.7 copy-start.6
  163.6 0.7 copy-start.7
  194.0 53.9 %copy-start = (bf16[128,2048]{1,0:T(8,128)(2,1)}, bf16[128,2048]{1,0:T(8,128)(2,1)S(1)}, u32[]{:S(2)}) copy-start(bf16[128,2048]{1,0:T(8,128)(2,1)S(1)} %reshape.509) | copy-start | bytes 1572868
  256.2 15.7 %collective-permute-start.5 = (bf16[16,1024]{1,0:T(8,128)(2,1)S(1)}, bf16[16,1024]{1,0:T(8,128)(2,1)S(1)}, u32[]{:S(2)}, u32[]{:S(2)}) collective-permute-start(bf16[16,1024]{1,0:T(8,128)(2,1)S(1)} %convolution_convert_fusion.6), channel_id=1, source_target_pairs={{6,0},{8,2},{10,4},{12,6},{14,8},{7,1},{9,3},{11,5},{13,7},{15,9},... | collective-permute-start | bytes 98312 | tf_op jit(solution)/shard_map/ppermute | solution.py:17
  259.7 14.1 %collective-permute-start.6 = (bf16[16,1024]{1,0:T(8,128)(2,1)S(1)}, bf16[16,1024]{1,0:T(8,128)(2,1)S(1)}, u32[]{:S(2)}, u32[]{:S(2)}) collective-permute-start(bf16[16,1024]{1,0:T(8,128)(2,1)S(1)} %convolution_convert_fusion.5), channel_id=1, source_target_pairs={{4,0},{6,2},{8,4},{10,6},{12,8},{14,10},{5,1},{7,3},{9,5},{11,7},{... | collective-permute-start | bytes 98312 | tf_op jit(solution)/shard_map/ppermute | solution.py:17
  261.8 12.1 %collective-permute-start.7 = (bf16[16,1024]{1,0:T(8,128)(2,1)S(1)}, bf16[16,1024]{1,0:T(8,128)(2,1)S(1)}, u32[]{:S(2)}, u32[]{:S(2)}) collective-permute-start(bf16[16,1024]{1,0:T(8,128)(2,1)S(1)} %convolution_convert_fusion.4), channel_id=1, source_target_pairs={{2,0},{4,2},{6,4},{8,6},{10,8},{12,10},{14,12},{3,1},{5,3},{7,5},{... | collective-permute-start | bytes 98312 | tf_op jit(solution)/shard_map/ppermute | solution.py:17
  264.1 9.7 %collective-permute-start.8 = (bf16[16,1024]{1,0:T(8,128)(2,1)S(1)}, bf16[16,1024]{1,0:T(8,128)(2,1)S(1)}, u32[]{:S(2)}, u32[]{:S(2)}) collective-permute-start(bf16[16,1024]{1,0:T(8,128)(2,1)S(1)} %convolution_convert_fusion.2), channel_id=1, source_target_pairs={{0,2},{2,4},{4,6},{6,8},{8,10},{10,12},{12,14},{1,3},{3,5},{5,7},{... | collective-permute-start | bytes 98312 | tf_op jit(solution)/shard_map/ppermute | solution.py:17
  267.9 6.0 %collective-permute-start.9 = (bf16[16,1024]{1,0:T(8,128)(2,1)S(1)}, bf16[16,1024]{1,0:T(8,128)(2,1)S(1)}, u32[]{:S(2)}, u32[]{:S(2)}) collective-permute-start(bf16[16,1024]{1,0:T(8,128)(2,1)S(1)} %convolution_convert_fusion.1), channel_id=1, source_target_pairs={{0,4},{2,6},{4,8},{6,10},{8,12},{10,14},{1,5},{3,7},{5,9},{7,11},{... | collective-permute-start | bytes 98312 | tf_op jit(solution)/shard_map/ppermute | solution.py:17
  271.9 7.6 %collective-permute-start.10 = (bf16[16,1024]{1,0:T(8,128)(2,1)S(1)}, bf16[16,1024]{1,0:T(8,128)(2,1)S(1)}, u32[]{:S(2)}, u32[]{:S(2)}) collective-permute-start(bf16[16,1024]{1,0:T(8,128)(2,1)S(1)} %convolution_convert_fusion), channel_id=1, source_target_pairs={{0,6},{2,8},{4,10},{6,12},{8,14},{1,7},{3,9},{5,11},{7,13},{9,15},... | collective-permute-start | bytes 98312 | tf_op jit(solution)/shard_map/ppermute | solution.py:17
Sparse Core Ops, SparseCore 0:
  19.1 79.8 all-reduce.2
  101.1 140.1 all-gather.1
  248.1 7.0 reduce-scatter.1
where the time goes:
time: 288 us; the launch traced here: 287 us
  waiting for transfers between devices  176 us (61%)
  starting transfers between devices  32.3 us (11%)
  other arithmetic  19.6 us (7%)
  between operations  19.3 us (7%)
  local copies, waits for them, and re-layouts  18.6 us (6%)
  matrix products  16.2 us (6%)
  loops' own time  5.19 us (2%)
    ppermute x11, waiting for transfers between devices, shifted_2(): return lax.ppermute(x, axis, pairs)  102 us
    all_gather x1, waiting for transfers between devices, local(): lax.all_gather(out_weight, 'ctx', axis=0, tiled=True)  46.6 us
    ppermute x11, starting transfers between devices, shifted_2(): return lax.ppermute(x, axis, pairs)  32.2 us
    psum x1, waiting for transfers between devices, broadcast(): return lax.psum(jnp.where(mine, x, jnp.zeros_like(x)), axis)  21.4 us
    and x4, other arithmetic, attend(): allowed = jnp.tile(allowed & (key_pos >= 0)[None, :], (group_width, 1))  7.95 us
    dot_general x1, matrix products, local(): lax.dot_general(selected, lax.all_gather(out_weight, 'ctx', axis=0, tiled...  6.71 us
    unnamed x38, local copies, waits for them, and re-layouts  6.43 us
  transfers between devices with their start and end apart: 14, of which 9 were waited for; matrix products, arithmetic and copies ran while one was open for 13% of the time, Pallas kernels for 0%

commit v1 on v0

--- a/solution.py
+++ b/solution.py
@@ -19,7 +19,7 @@
 
 def broadcast(x, axis, root):
     mine = lax.axis_index(axis) == root
-    return lax.psum(jnp.where(mine, x, jnp.zeros_like(x)), axis)
+    return jnp.sum(lax.all_gather(jnp.where(mine, x, jnp.zeros_like(x)), axis), axis=0)
 
 
 def attend(

time: 288 us -> 441 us (1.53)
  blocking collectives: 0 us -> 278 us
  waiting for transfers between devices: 176 us -> 53 us
    all_gather x0 -> x8, blocking collectives: none -> 278 us  [broadcast(): lax.all_gather(jnp.where(mine, x, jnp.zeros_like(x)), axis)]
    ppermute x11, waiting for transfers between devices: 102 us -> 45.1 us  [shifted_2(): return lax.ppermute(x, axis, pairs)]
    all_gather x1, waiting for transfers between devices: 46.6 us -> 0.02 us  [local(): lax.all_gather(out_weight, 'ctx', axis=0, tiled=True)]
    psum x1 -> x0, waiting for transfers between devices: 21.4 us -> none  [broadcast(): return lax.psum(jnp.where(mine, x, jnp.zeros_like(x)), axis)]
  transfers between devices with their start and end apart: 14 -> 13, of which waited for: 9 -> 6; matrix products, arithmetic and copies ran while one was open for 13% -> 8% of each run, Pallas kernels for 0% -> 0%
where the time goes in v1:
time: 441 us; the launch traced here: 440 us
  blocking collectives  278 us (63%)
  waiting for transfers between devices  53 us (12%)
  starting transfers between devices  34.7 us (8%)
  between operations  19.7 us (4%)
  local copies, waits for them, and re-layouts  16.7 us (4%)
  other arithmetic  16.4 us (4%)
  matrix products  16.2 us (4%)
  loops' own time  4.87 us (1%)
    all_gather x8, blocking collectives, broadcast(): lax.all_gather(jnp.where(mine, x, jnp.zeros_like(x)), axis)  278 us
    ppermute x11, waiting for transfers between devices, shifted_2(): return lax.ppermute(x, axis, pairs)  45.1 us
    ppermute x11, starting transfers between devices, shifted_2(): return lax.ppermute(x, axis, pairs)  34.6 us
  transfers between devices with their start and end apart: 13, of which 6 were waited for; matrix products, arithmetic and copies ran while one was open for 8% of the time, Pallas kernels for 0%

profile of v1, /device:TPU:16, one launch (start us, length us, event | category | flops | bytes accessed | tf_op | source)
XLA Modules:
  0.0 440.1 jit_solution(6534106461066555555)
XLA Ops:
  9.4 3.4 collective-permute-start
  16.4 42.1 %all_gather.35 = bf16[8,2,128,128]{3,2,1,0:T(8,128)(2,1)S(1)} all-gather(bf16[1,2,128,128]{3,2,1,0:T(8,128)(2,1)S(1)} %copy.147), channel_id=1, replica_groups=mesh['groups'=2,'ctx'=8,'head'=2] {'ctx'}, dimensions={0}, use_global_device_ids=true | all-gather | bytes 589824 | tf_op jit(solution)/shard_map/all_gather | solution.py:22
  58.8 32.3 %all_gather.36 = bf16[8,2,128,128]{3,2,1,0:T(8,128)(2,1)S(1)} all-gather(bf16[1,2,128,128]{3,2,1,0:T(8,128)(2,1)S(1)} %copy.149), channel_id=1, replica_groups=mesh['groups'=2,'ctx'=8,'head'=2] {'ctx'}, dimensions={0}, use_global_device_ids=true | all-gather | bytes 589824 | tf_op jit(solution)/shard_map/all_gather | solution.py:22
  91.3 32.7 %all_gather.37 = bf16[8,2,128,128]{3,2,1,0:T(8,128)(2,1)S(1)} all-gather(bf16[1,2,128,128]{3,2,1,0:T(8,128)(2,1)S(1)} %copy.151), channel_id=1, replica_groups=mesh['groups'=2,'ctx'=8,'head'=2] {'ctx'}, dimensions={0}, use_global_device_ids=true | all-gather | bytes 589824 | tf_op jit(solution)/shard_map/all_gather | solution.py:22
  124.2 33.2 %all_gather.38 = bf16[8,2,128,128]{3,2,1,0:T(8,128)(2,1)S(1)} all-gather(bf16[1,2,128,128]{3,2,1,0:T(8,128)(2,1)S(1)} %copy.153), channel_id=1, replica_groups=mesh['groups'=2,'ctx'=8,'head'=2] {'ctx'}, dimensions={0}, use_global_device_ids=true | all-gather | bytes 589824 | tf_op jit(solution)/shard_map/all_gather | solution.py:22
  160.2 30.0 %all_gather.39 = bf16[8,2,128,128]{3,2,1,0:T(8,128)(2,1)S(1)} all-gather(bf16[1,2,128,128]{3,2,1,0:T(8,128)(2,1)S(1)} %copy.155), channel_id=1, replica_groups=mesh['groups'=2,'ctx'=8,'head'=2] {'ctx'}, dimensions={0}, use_global_device_ids=true | all-gather | bytes 589824 | tf_op jit(solution)/shard_map/all_gather | solution.py:22
  191.1 31.6 %all_gather.40 = bf16[8,2,128,128]{3,2,1,0:T(8,128)(2,1)S(1)} all-gather(bf16[1,2,128,128]{3,2,1,0:T(8,128)(2,1)S(1)} %copy.157), channel_id=1, replica_groups=mesh['groups'=2,'ctx'=8,'head'=2] {'ctx'}, dimensions={0}, use_global_device_ids=true | all-gather | bytes 589824 | tf_op jit(solution)/shard_map/all_gather | solution.py:22
  223.0 31.0 %all_gather.41 = bf16[8,2,128,128]{3,2,1,0:T(8,128)(2,1)S(1)} all-gather(bf16[1,2,128,128]{3,2,1,0:T(8,128)(2,1)S(1)} %copy.161), channel_id=1, replica_groups=mesh['groups'=2,'ctx'=8,'head'=2] {'ctx'}, dimensions={0}, use_global_device_ids=true | all-gather | bytes 589824 | tf_op jit(solution)/shard_map/all_gather | solution.py:22
  254.3 45.5 %all_gather.42 = bf16[8,2,128,128]{3,2,1,0:T(8,128)(2,1)S(1)} all-gather(bf16[1,2,128,128]{3,2,1,0:T(8,128)(2,1)S(1)} %copy.163), channel_id=1, replica_groups=mesh['groups'=2,'ctx'=8,'head'=2] {'ctx'}, dimensions={0}, use_global_device_ids=true | all-gather | bytes 589824 | tf_op jit(solution)/shard_map/all_gather | solution.py:22
  301.5 4.7 %collective-permute-start.1 = (bf16[4,128,4,128]{3,1,2,0:T(8,128)(2,1)S(1)}, bf16[4,128,4,128]{3,1,2,0:T(8,128)(2,1)S(1)}, u32[]{:S(2)}, u32[]{:S(2)}) collective-permute-start(bf16[4,128,4,128]{3,1,2,0:T(8,128)(2,1)S(1)} %broadcast_select_fusion), channel_id=1, source_target_pairs={{0,4},{2,6},{4,8},{6,10},{8,12},{10,14},{1,5},{3,7},{5,9},{7,11},{... | collective-permute-start | bytes 1572872 | tf_op jit(solution)/shard_map/ppermute | solution.py:17
  306.2 6.6 %collective-permute-done.1 = bf16[4,128,4,128]{3,1,2,0:T(8,128)(2,1)S(1)} collective-permute-done((bf16[4,128,4,128]{3,1,2,0:T(8,128)(2,1)S(1)}, bf16[4,128,4,128]{3,1,2,0:T(8,128)(2,1)S(1)}, u32[]{:S(2)}, u32[]{:S(2)}) %collective-permute-start.1) | collective-permute-done | bytes 524320 | tf_op jit(solution)/shard_map/ppermute | solution.py:17
  313.0 1.3 collective-permute-start.2
  314.4 10.7 %collective-permute-done.2 = bf16[4,128,4,128]{3,1,2,0:T(8,128)(2,1)S(1)} collective-permute-done((bf16[4,128,4,128]{3,1,2,0:T(8,128)(2,1)S(1)}, bf16[4,128,4,128]{3,1,2,0:T(8,128)(2,1)S(1)}, u32[]{:S(2)}, u32[]{:S(2)}) %collective-permute-start.2) | collective-permute-done | bytes 524320 | tf_op jit(solution)/shard_map/ppermute | solution.py:17
  325.3 6.1 %collective-permute-start.3 = (bf16[6,128,4,128]{3,1,2,0:T(8,128)(2,1)S(1)}, bf16[6,128,4,128]{3,1,2,0:T(8,128)(2,1)S(1)}, u32[]{:S(2)}, u32[]{:S(2)}) collective-permute-start(bf16[6,128,4,128]{3,1,2,0:T(8,128)(2,1)S(1)} %get-tuple-element.226), channel_id=1, source_target_pairs={{0,2},{2,4},{4,6},{6,8},{8,10},{10,12},{12,14},{1,3},{3,5},{5,7},{... | collective-permute-start | bytes 2359304 | tf_op jit(solution)/shard_map/ppermute | solution.py:17
  333.7 11.3 %collective-permute-done.3 = bf16[6,128,4,128]{3,1,2,0:T(8,128)(2,1)S(1)} collective-permute-done((bf16[6,128,4,128]{3,1,2,0:T(8,128)(2,1)S(1)}, bf16[6,128,4,128]{3,1,2,0:T(8,128)(2,1)S(1)}, u32[]{:S(2)}, u32[]{:S(2)}) %collective-permute-start.3) | collective-permute-done | bytes 786464 | tf_op jit(solution)/shard_map/ppermute | solution.py:17
  345.0 2.2 collective-permute-start.4
  348.9 10.8 %collective-permute-done.4 = bf16[6,128,4,128]{3,1,2,0:T(8,128)(2,1)S(1)} collective-permute-done((bf16[6,128,4,128]{3,1,2,0:T(8,128)(2,1)S(1)}, bf16[6,128,4,128]{3,1,2,0:T(8,128)(2,1)S(1)}, u32[]{:S(2)}, u32[]{:S(2)}) %collective-permute-start.4) | collective-permute-done | bytes 786464 | tf_op jit(solution)/shard_map/ppermute | solution.py:17
  361.9 27.3 %while.13 = (s32[]{:T(128)}, bf16[4,512,128]{2,1,0:T(8,128)(2,1)}, s32[4,1408]{1,0:T(4,128)S(1)}, s32[4,2]{1,0:T(4,128)S(1)}, s32[4,2]{0,1:T(2,128)S(1)}, /*inde...) while((s32[]{:T(128)}, bf16[4,512,128]{2,1,0:T(8,128)(2,1)}, ...), condition=%wide.region_12.13_spmd.clone, body=%wide.region_8.12_spmd.clone.sunk | while | flops 378271104 | bytes 10238073 | solution.py:193
  364.0 1.9 fusion.119
  370.8 1.9 fusion.119
  377.6 1.9 fusion.119
  384.4 1.9 fusion.119
  389.2 1.4 copy.204
  391.7 6.7 %fusion.32 = f32[32,2048]{1,0:T(8,128)} fusion(bf16[2048,2048]{1,0:T(8,128)(2,1)} %all-gather.2.cloned.1.call-done, bf16[32,2048]{1,0:T(8,128)(2,1)S(1)} %gather_fusion, pred[32]{0:T(512)(128)(4,1)S(1)} %compare_and_fusion), kind=kOutput, calls=%fused_computation.75 | convolution fusion | flops 268500992 | bytes 8781856 | tf_op jit(solution)/shard_map/dot_general | solution.py:212
  400.3 7.9 %reduce-scatter.2.cloned.1.call-done = f32[32,1024]{1,0:T(8,128)} async-done(((f32[32,2048]{1,0:T(8,128)}), f32[32,1024]{1,0:T(8,128)}) %reduce-scatter.2.cloned.1.call-update) | async-done | bytes 131088 | tf_op jit(solution)/shard_map/reduce_scatter | solution.py:211
  409.2 3.3 collective-permute-start.5
  412.7 1.9 collective-permute-start.6
  414.7 2.2 collective-permute-start.7
  417.1 3.6 collective-permute-start.8
  420.9 3.9 collective-permute-start.9
  424.9 1.9 collective-permute-start.10
  426.9 5.6 %collective-permute-done.10 = bf16[16,1024]{1,0:T(8,128)(2,1)S(1)} collective-permute-done((bf16[16,1024]{1,0:T(8,128)(2,1)S(1)}, bf16[16,1024]{1,0:T(8,128)(2,1)S(1)}, u32[]{:S(2)}, u32[]{:S(2)}) %collective-permute-start.10) | collective-permute-done | bytes 32800 | tf_op jit(solution)/shard_map/ppermute | solution.py:17
  (208 shorter events, 33.6 us)
Async XLA Ops:
  7.2 5.7 %copy-start.4 = (bf16[128,512]{1,0:T(8,128)(2,1)S(1)}, bf16[128,512]{1,0:T(8,128)(2,1)}, u32[]{:S(2)}) copy-start(bf16[128,512]{1,0:T(8,128)(2,1)} %param.11) | copy-start | bytes 393220
  7.2 5.8 %copy-start.5 = (bf16[128,512]{1,0:T(8,128)(2,1)S(1)}, bf16[128,512]{1,0:T(8,128)(2,1)}, u32[]{:S(2)}) copy-start(bf16[128,512]{1,0:T(8,128)(2,1)} %param.12) | copy-start | bytes 393220
  7.2 6.0 %copy-start.9 = (s32[4,2]{0,1:T(2,128)S(1)}, s32[4,2]{0,1:T(2,128)}, u32[]{:S(2)}) copy-start(s32[4,2]{0,1:T(2,128)} %param.14) | copy-start | bytes 100
  7.2 384.5 %all-gather.2.cloned.1.call-start = ((), (), s32[]{:S(2)}) async-start(), calls=%async_computation.1 | async-start | bytes 9437184 | tf_op jit(solution)/shard_map/all_gather | solution.py:214
  9.4 292.0 %collective-permute-start = (bf16[4,128,4,128]{3,1,2,0:T(8,128)(2,1)S(1)}, bf16[4,128,4,128]{3,1,2,0:T(8,128)(2,1)S(1)}, u32[]{:S(2)}, u32[]{:S(2)}) collective-permute-start(bf16[4,128,4,128]{3,1,2,0:T(8,128)(2,1)S(1)} %get-tuple-element.228), channel_id=1, source_target_pairs={{0,2},{2,4},{4,6},{6,8},{8,10},{10,12},{12,14},{1,3},{3,5},{5,7},{... | collective-permute-start | bytes 1572872 | tf_op jit(solution)/shard_map/ppermute | solution.py:17
  12.8 395.4 %reduce-scatter.2.cloned.1.call-start = ((), (), s32[]{:S(2)}) async-start(), calls=%async_computation.2 | async-start | bytes 393216 | tf_op jit(solution)/shard_map/reduce_scatter | solution.py:211
  191.1 110.0 %copy-start.10 = (s32[4,2]{0,1:T(2,128)S(1)}, s32[4,2]{0,1:T(2,128)}, u32[]{:S(2)}) copy-start(s32[4,2]{0,1:T(2,128)} %param.13) | copy-start | bytes 100
  254.0 52.2 %copy-start.11 = (s32[1,32]{1,0:T(1,128)S(1)}, s32[1,32]{1,0:T(1,128)}, u32[]{:S(2)}) copy-start(s32[1,32]{1,0:T(1,128)} %param.15) | copy-start | bytes 388
  301.5 11.4 %collective-permute-start.1 = (bf16[4,128,4,128]{3,1,2,0:T(8,128)(2,1)S(1)}, bf16[4,128,4,128]{3,1,2,0:T(8,128)(2,1)S(1)}, u32[]{:S(2)}, u32[]{:S(2)}) collective-permute-start(bf16[4,128,4,128]{3,1,2,0:T(8,128)(2,1)S(1)} %broadcast_select_fusion), channel_id=1, source_target_pairs={{0,4},{2,6},{4,8},{6,10},{8,12},{10,14},{1,5},{3,7},{5,9},{7,11},{... | collective-permute-start | bytes 1572872 | tf_op jit(solution)/shard_map/ppermute | solution.py:17
  313.0 12.1 %collective-permute-start.2 = (bf16[4,128,4,128]{3,1,2,0:T(8,128)(2,1)S(1)}, bf16[4,128,4,128]{3,1,2,0:T(8,128)(2,1)S(1)}, u32[]{:S(2)}, u32[]{:S(2)}) collective-permute-start(bf16[4,128,4,128]{3,1,2,0:T(8,128)(2,1)S(1)} %broadcast_select_fusion.1), channel_id=1, source_target_pairs={{0,8},{2,10},{4,12},{6,14},{1,9},{3,11},{5,13},{7,15},{16,24},{18,... | collective-permute-start | bytes 1572872 | tf_op jit(solution)/shard_map/ppermute | solution.py:17
  325.1 8.4 %copy-start.12 = (s32[8]{0:T(128)S(1)}, s32[8]{0:T(128)}, u32[]{:S(2)}) copy-start(s32[8]{0:T(128)} %param.16) | copy-start | bytes 100
  325.1 22.2 %copy-start.3 = (bf16[128,2048]{1,0:T(8,128)(2,1)S(1)}, bf16[128,2048]{1,0:T(8,128)(2,1)}, u32[]{:S(2)}) copy-start(bf16[128,2048]{1,0:T(8,128)(2,1)} %param.10) | copy-start | bytes 1572868
  325.3 19.7 %collective-permute-start.3 = (bf16[6,128,4,128]{3,1,2,0:T(8,128)(2,1)S(1)}, bf16[6,128,4,128]{3,1,2,0:T(8,128)(2,1)S(1)}, u32[]{:S(2)}, u32[]{:S(2)}) collective-permute-start(bf16[6,128,4,128]{3,1,2,0:T(8,128)(2,1)S(1)} %get-tuple-element.226), channel_id=1, source_target_pairs={{0,2},{2,4},{4,6},{6,8},{8,10},{10,12},{12,14},{1,3},{3,5},{5,7},{... | collective-permute-start | bytes 2359304 | tf_op jit(solution)/shard_map/ppermute | solution.py:17
  345.0 14.8 %collective-permute-start.4 = (bf16[6,128,4,128]{3,1,2,0:T(8,128)(2,1)S(1)}, bf16[6,128,4,128]{3,1,2,0:T(8,128)(2,1)S(1)}, u32[]{:S(2)}, u32[]{:S(2)}) collective-permute-start(bf16[6,128,4,128]{3,1,2,0:T(8,128)(2,1)S(1)} %collective-permute-done.3), channel_id=1, source_target_pairs={{0,2},{2,4},{4,6},{6,8},{8,10},{10,12},{12,14},{1,3},{3,5},{5,7},{... | collective-permute-start | bytes 2359304 | tf_op jit(solution)/shard_map/ppermute | solution.py:17
  360.2 1.0 copy-start.2
  360.2 1.0 copy-start.1
  361.2 0.7 copy-start.6
  361.2 0.7 copy-start.7
  361.2 0.7 copy-start.8
  391.0 7.4 %copy-start = (bf16[128,2048]{1,0:T(8,128)(2,1)}, bf16[128,2048]{1,0:T(8,128)(2,1)S(1)}, u32[]{:S(2)}) copy-start(bf16[128,2048]{1,0:T(8,128)(2,1)S(1)} %reshape.757) | copy-start | bytes 1572868
  409.2 15.7 %collective-permute-start.5 = (bf16[16,1024]{1,0:T(8,128)(2,1)S(1)}, bf16[16,1024]{1,0:T(8,128)(2,1)S(1)}, u32[]{:S(2)}, u32[]{:S(2)}) collective-permute-start(bf16[16,1024]{1,0:T(8,128)(2,1)S(1)} %convolution_convert_fusion.6), channel_id=1, source_target_pairs={{6,0},{8,2},{10,4},{12,6},{14,8},{7,1},{9,3},{11,5},{13,7},{15,9},... | collective-permute-start | bytes 98312 | tf_op jit(solution)/shard_map/ppermute | solution.py:17
  412.7 14.1 %collective-permute-start.6 = (bf16[16,1024]{1,0:T(8,128)(2,1)S(1)}, bf16[16,1024]{1,0:T(8,128)(2,1)S(1)}, u32[]{:S(2)}, u32[]{:S(2)}) collective-permute-start(bf16[16,1024]{1,0:T(8,128)(2,1)S(1)} %convolution_convert_fusion.5), channel_id=1, source_target_pairs={{4,0},{6,2},{8,4},{10,6},{12,8},{14,10},{5,1},{7,3},{9,5},{11,7},{... | collective-permute-start | bytes 98312 | tf_op jit(solution)/shard_map/ppermute | solution.py:17
  414.7 12.1 %collective-permute-start.7 = (bf16[16,1024]{1,0:T(8,128)(2,1)S(1)}, bf16[16,1024]{1,0:T(8,128)(2,1)S(1)}, u32[]{:S(2)}, u32[]{:S(2)}) collective-permute-start(bf16[16,1024]{1,0:T(8,128)(2,1)S(1)} %convolution_convert_fusion.4), channel_id=1, source_target_pairs={{2,0},{4,2},{6,4},{8,6},{10,8},{12,10},{14,12},{3,1},{5,3},{7,5},{... | collective-permute-start | bytes 98312 | tf_op jit(solution)/shard_map/ppermute | solution.py:17
  417.1 9.7 %collective-permute-start.8 = (bf16[16,1024]{1,0:T(8,128)(2,1)S(1)}, bf16[16,1024]{1,0:T(8,128)(2,1)S(1)}, u32[]{:S(2)}, u32[]{:S(2)}) collective-permute-start(bf16[16,1024]{1,0:T(8,128)(2,1)S(1)} %convolution_convert_fusion.2), channel_id=1, source_target_pairs={{0,2},{2,4},{4,6},{6,8},{8,10},{10,12},{12,14},{1,3},{3,5},{5,7},{... | collective-permute-start | bytes 98312 | tf_op jit(solution)/shard_map/ppermute | solution.py:17
  420.9 6.0 %collective-permute-start.9 = (bf16[16,1024]{1,0:T(8,128)(2,1)S(1)}, bf16[16,1024]{1,0:T(8,128)(2,1)S(1)}, u32[]{:S(2)}, u32[]{:S(2)}) collective-permute-start(bf16[16,1024]{1,0:T(8,128)(2,1)S(1)} %convolution_convert_fusion.1), channel_id=1, source_target_pairs={{0,4},{2,6},{4,8},{6,10},{8,12},{10,14},{1,5},{3,7},{5,9},{7,11},{... | collective-permute-start | bytes 98312 | tf_op jit(solution)/shard_map/ppermute | solution.py:17
  424.9 7.6 %collective-permute-start.10 = (bf16[16,1024]{1,0:T(8,128)(2,1)S(1)}, bf16[16,1024]{1,0:T(8,128)(2,1)S(1)}, u32[]{:S(2)}, u32[]{:S(2)}) collective-permute-start(bf16[16,1024]{1,0:T(8,128)(2,1)S(1)} %convolution_convert_fusion), channel_id=1, source_target_pairs={{0,6},{2,8},{4,10},{6,12},{8,14},{1,7},{3,9},{5,11},{7,13},{9,15},... | collective-permute-start | bytes 98312 | tf_op jit(solution)/shard_map/ppermute | solution.py:17
Sparse Core Ops, SparseCore 0:
  12.9 154.2 all-gather.1
  398.6 9.5 reduce-scatter.1
